TPU v7x, 512 devices: a whole 4x8x8 slice. The times are simulated.
512 devices in a mesh: dp: 128 (over y, x, z_lo, core), strip: 4 (over z_hi).
Axes of the slice: x: 4, y: 8, z: 8 (z_hi: 4, z_lo: 2; z = z_hi * 2 + z_lo), core: 2. Of those that a mesh axis runs over, the one named last changes fastest.
Arguments:
- latents: bfloat16 [128, 4, 320, 128], P('dp', 'strip'), may hold values from -6 to 6
- cotangent: bfloat16 [128, 4, 320, 128], P('dp', 'strip'), may hold values from -16 to 16
- weight: bfloat16 [320, 2880], P('strip'), may hold values from -0.109375 to 0.109375
- master: float32 [512, 2880], P('dp'), may hold values from -0.21875 to 0.21875
- first_moment: float32 [512, 2880], P('dp'), may hold values from -6 to 6
- second_moment: float32 [512, 2880], P('dp'), may hold values from 0.005 to 0.05
- owner_list: int32 [320], replicated, may hold values from 0 to 127, as said below
Outputs:
- output: bfloat16 [128, 4, 320, 128], P('dp', 'strip')
- grad_input: bfloat16 [128, 4, 320, 128], P('dp', 'strip')
- new_weight: bfloat16 [320, 2880], P('strip')
- new_master: float32 [512, 2880], P('dp')
- new_first: float32 [512, 2880], P('dp')
- new_second: float32 [512, 2880], P('dp')
Inputs may be any that keep to these rules, and one draw needn't show every extreme that they name: `owner_list`: each of the 128 ranks owns at least one and at most 4 buckets, and some rank owns exactly 4.
All inputs are finite; a program needn't handle non-finite values.
Results may differ from a plain program's by a relative error of at most 0.0033.
Values may be sent and summed in bfloat16 or wider, within the bound.
No kernel may reach another device: no remote copies, remote signals or barrier semaphores. Data moves between devices by JAX's collectives and lax.ppermute only.
A program may use at most 64 MiB of HBM per device.

v0:
```python
import jax
import jax.numpy as jnp
from jax import lax
from jax.sharding import PartitionSpec as P

beta_first = 0.9
beta_second = 0.999
learn_rate = 0.01
epsilon = 1e-08
bias_first = 1.0 - 0.9**10
bias_second = 1.0 - 0.999**10


def extended(cells, sides, width):
    for axis, dim in sides:
        count = lax.axis_size(axis)
        ends = count - 1
        head = lax.slice_in_dim(cells, 0, width, axis=dim)
        tail = lax.slice_in_dim(cells, cells.shape[dim] - width, cells.shape[dim], axis=dim)
        cells = jnp.concatenate(
            [
                lax.ppermute(tail, axis, [(i, (i + 1) % count) for i in range(ends)]),
                cells,
                lax.ppermute(head, axis, [((i + 1) % count, i) for i in range(ends)]),
            ],
            axis=dim,
        )
    return cells


def patches(padded, direction):
    widened = jnp.pad(padded, ((0, 0), (0, 0), (1, 1)))
    height = padded.shape[0] - 2
    across = padded.shape[2]
    pieces = []
    for row_step in (-1, 0, 1):
        for col_step in (-1, 0, 1):
            row_start = 1 + direction * row_step
            col_start = 1 + direction * col_step
            pieces.append(
                widened[row_start : row_start + height, :, col_start : col_start + across]
            )
    return jnp.concatenate(pieces, axis=1)


def flipped(weight):
    channels = weight.shape[0]
    return weight.reshape(channels, 9, channels).transpose(2, 1, 0).reshape(channels, 9 * channels)


def slot_tables(owner_list, capacity):
    count = owner_list.shape[0]
    same_owner = owner_list[:, None] == owner_list[None, :]
    earlier = (
        jnp.arange(count, dtype=jnp.int32)[None, :] < jnp.arange(count, dtype=jnp.int32)[:, None]
    )
    within = jnp.sum((same_owner & earlier).astype(jnp.int32), axis=1)
    return owner_list * capacity + within


def adam_update(grads, master, first_moment, second_moment, filled):
    first_new = beta_first * first_moment + (1.0 - beta_first) * grads
    second_new = beta_second * second_moment + (1.0 - beta_second) * grads * grads
    update = learn_rate * (first_new / bias_first) / (jnp.sqrt(second_new / bias_second) + epsilon)
    keep = filled[:, None]
    return (
        jnp.where(keep, master - update, master),
        jnp.where(keep, first_new, first_moment),
        jnp.where(keep, second_new, second_moment),
    )


def local(latents, cotangent, weight, master, first_moment, second_moment, owner_list):
    full_weight = lax.all_gather(weight, "strip", axis=0, tiled=True)
    channels = full_weight.shape[0]
    pixels = latents[0]
    upstream = cotangent[0]
    pixels_float = pixels.astype(jnp.float32)
    active = jax.nn.silu(pixels_float).astype(jnp.bfloat16)
    active_rim = extended(active, (("strip", 0),), 1)
    forward_cols = patches(active_rim, 1)
    convolved = jnp.einsum(
        "ok,hkw->how", full_weight, forward_cols, preferred_element_type=jnp.float32
    )
    output = (pixels_float + convolved).astype(jnp.bfloat16)
    upstream_rim = extended(upstream, (("strip", 0),), 1)
    backward_cols = patches(upstream_rim, -1)
    spread = jnp.einsum(
        "ck,hkw->hcw", flipped(full_weight), backward_cols, preferred_element_type=jnp.float32
    )
    sigmoid_val = jax.nn.sigmoid(pixels_float)
    derivative = sigmoid_val * (1.0 + pixels_float * (1.0 - sigmoid_val))
    grad_input = (upstream.astype(jnp.float32) + spread * derivative).astype(jnp.bfloat16)
    partial_grad = jnp.einsum(
        "how,hkw->ok", upstream, forward_cols, preferred_element_type=jnp.float32
    )
    capacity = master.shape[0]
    owners = lax.axis_size("dp")
    owner_rank = lax.axis_index("dp")
    slot_ids = slot_tables(owner_list, capacity)
    matches = slot_ids[None, :] == jnp.arange(owners * capacity, dtype=jnp.int32)[:, None]
    bucket = jnp.sum(jnp.where(matches, jnp.arange(channels, dtype=jnp.int32)[None, :], 0), axis=1)
    filled = jnp.any(matches, axis=1)
    source_row = jnp.where(filled, bucket, channels)
    my_filled = lax.dynamic_slice_in_dim(filled, owner_rank * capacity, capacity)
    outgoing = jnp.take(partial_grad, source_row, axis=0, mode="fill", fill_value=0.0).reshape(
        owners, capacity, 9 * channels
    )
    incoming = lax.all_to_all(
        outgoing.astype(jnp.bfloat16), "dp", split_axis=0, concat_axis=0, tiled=True
    ).astype(outgoing.dtype)
    owned_grad = lax.psum(jnp.sum(incoming, axis=0).astype(jnp.bfloat16), "strip").astype(
        jnp.float32
    )
    pixel_count = (
        latents.shape[0] * owners * pixels.shape[0] * lax.axis_size("strip") * pixels.shape[2]
    )
    gradient = owned_grad / jnp.sqrt(jnp.float32(pixel_count))
    new_master, new_first, new_second = adam_update(
        gradient, master, first_moment, second_moment, my_filled
    )
    published = lax.all_gather(new_master.astype(jnp.bfloat16), "dp", axis=0, tiled=True)
    quarter = weight.shape[0]
    wanted = lax.dynamic_slice_in_dim(slot_ids, lax.axis_index("strip") * quarter, quarter)
    new_weight = published[wanted]
    return (output[None], grad_input[None], new_weight, new_master, new_first, new_second)


def solution(mesh):
    in_specs = (
        P("dp", "strip", None, None),
        P("dp", "strip", None, None),
        P("strip", None),
        P("dp", None),
        P("dp", None),
        P("dp", None),
        P(),
    )
    out_specs = (
        P("dp", "strip", None, None),
        P("dp", "strip", None, None),
        P("strip", None),
        P("dp", None),
        P("dp", None),
        P("dp", None),
    )
    return jax.shard_map(local, mesh=mesh, in_specs=in_specs, out_specs=out_specs, check_vma=False)
```

profile of v0, /device:TPU:8, one launch (start us, length us, event | category | flops | bytes accessed | tf_op | source)
XLA Modules:
  0.0 371.5 jit_solution(15134228021462257407)
XLA Ops:
  7.2 0.9 fusion.17
  8.1 1.3 collective-permute-start.1
  9.4 6.7 %collective-permute-start = (bf16[1,320,128]{2,1,0:T(8,128)(2,1)S(1)}, bf16[1,320,128]{2,1,0:T(8,128)(2,1)S(1)}, u32[]{:S(2)}, u32[]{:S(2)}) collective-permute-start(bf16[1,320,128]{2,1,0:T(8,128)(2,1)S(1)} %fusion.17), channel_id=1, source_target_pairs={{0,1},{1,2},{2,3},{4,5},{5,6},{6,7},{8,9},{9,10},{10,11},{12,13},{... | collective-permute-start | bytes 245768 | tf_op jit(solution)/shard_map/ppermute | solution.py:22
  16.1 1.0 convert_reduce_fusion
  17.1 0.7 multiply_add_fusion
  17.8 0.2 fusion.11
  18.0 0.1 select_reduce_fusion
  18.1 0.1 select_n.68
  18.3 0.2 select_maximum_fusion.2
  18.6 0.1 slice_dynamic-update-slice_fusion.10
  18.7 1.0 constant_dynamic-update-slice_fusion.1
  19.7 0.1 slice_dynamic-update-slice_fusion.8
  19.8 0.1 slice_dynamic-update-slice_fusion.6
  20.0 0.8 copy-done.1
  20.8 1.5 convolution_bitcast_fusion
  22.4 3.7 gather_fusion
  26.1 4.7 %gather.10 = bf16[128,4,2880]{2,1,0:T(4,128)(2,1)S(1)} reshape(bf16[512,2880]{1,0:T(8,128)(2,1)} %gather_fusion) | data formatting | bytes 5898240 | tf_op jit(solution)/shard_map/jit(_take)/gather | solution.py:106
  30.7 3.7 select_convert_fusion
  34.4 13.5 %all-to-all-start = ((bf16[128,4,2880]{2,1,0:T(4,128)(2,1)}), bf16[128,4,2880]{2,1,0:T(4,128)(2,1)S(1)}, u32[]{:S(2)}, u32[]{:S(2)}) async-start(bf16[128,4,2880]{2,1,0:T(4,128)(2,1)} %select_convert_fusion), calls=%async_computation | async-start | bytes 6029312 | tf_op jit(solution)/shard_map/all_to_all | solution.py:109
  48.0 0.0 all-gather.4.cloned.1.call-start
  48.0 0.7 all-gather.4.cloned.1.call-update
  48.8 0.1 dynamic_slice.6
  48.9 69.2 %all-to-all-done = bf16[128,4,2880]{2,1,0:T(4,128)(2,1)S(1)} async-done(((bf16[128,4,2880]{2,1,0:T(4,128)(2,1)}), bf16[128,4,2880]{2,1,0:T(4,128)(2,1)S(1)}, u32[]{:S(2)}, u32[]{:S(2)}) %all-to-all-start) | async-done | bytes 2949152 | tf_op jit(solution)/shard_map/all_to_all | solution.py:109
  118.1 1.3 reduce_sum.32
  119.4 25.1 %psum.7 = bf16[4,2880]{1,0:T(4,128)(2,1)S(1)} all-reduce(bf16[4,2880]{1,0:T(4,128)(2,1)S(1)} %reduce_sum.32), channel_id=1, replica_groups=mesh['dp'=128,'strip'=4] {'strip'}, use_global_device_ids=true, to_apply=%region_4.5 | all-reduce | flops 11520 | bytes 46080 | tf_op jit(solution)/shard_map/psum | solution.py:112
  144.5 0.8 convert_bitcast_fusion
  145.3 1.3 collective-permute-start.3
  146.6 5.6 %collective-permute-start.2 = (bf16[1,320,128]{2,1,0:T(8,128)(2,1)S(1)}, bf16[1,320,128]{2,1,0:T(8,128)(2,1)S(1)}, u32[]{:S(2)}, u32[]{:S(2)}) collective-permute-start(bf16[1,320,128]{2,1,0:T(8,128)(2,1)S(1)} %bitcast.62), channel_id=1, source_target_pairs={{0,1},{1,2},{2,3},{4,5},{5,6},{6,7},{8,9},{9,10},{10,11},{12,13},{... | collective-permute-start | bytes 245768 | tf_op jit(solution)/shard_map/ppermute | solution.py:22
  152.3 0.1 compare_select_fusion.2
  152.4 0.2 collective-permute-done.3
  152.6 1.6 collective-permute-done.2
  154.1 0.2 select_maximum_fusion
  154.4 0.7 slice_dynamic-update-slice_fusion.5
  155.1 0.6 constant_dynamic-update-slice_fusion.5
  155.7 0.6 slice_dynamic-update-slice_fusion.4
  156.4 0.7 slice_dynamic-update-slice_fusion.3
  157.1 0.6 constant_dynamic-update-slice_fusion.4
  157.7 0.7 slice_dynamic-update-slice_fusion.2
  158.4 0.7 slice_dynamic-update-slice_fusion.1
  159.1 0.6 constant_dynamic-update-slice_fusion.3
  159.7 0.6 slice_dynamic-update-slice_fusion
  160.4 3.3 copy.17
  163.7 2.5 copy.18
  166.2 3.0 fusion.6
  169.2 2.7 fusion.5
  171.9 186.7 %all-gather.6.cloned.1.call-done = bf16[128,4,2880]{2,1,0:T(4,128)(2,1)} async-done(((bf16[1,4,2880]{2,1,0:T(4,128)(2,1)}), bf16[128,4,2880]{2,1,0:T(4,128)(2,1)}) %all-gather.6.cloned.1.call-update) | async-done | bytes 2949136 | tf_op jit(solution)/shard_map/all_gather | solution.py:122
  358.6 4.4 %reshape.171 = bf16[512,2880]{1,0:T(8,128)(2,1)S(1)} reshape(bf16[128,4,2880]{2,1,0:T(4,128)(2,1)} %all-gather.6.cloned.1.call-done) | data formatting | bytes 5898240
  363.0 1.6 gather_fusion.1
  (30 shorter events, 0.2 us)
Async XLA Ops:
  8.1 10.2 %collective-permute-start.1 = (bf16[1,320,128]{2,1,0:T(8,128)(2,1)S(1)}, bf16[1,320,128]{2,1,0:T(8,128)(2,1)S(1)}, u32[]{:S(2)}, u32[]{:S(2)}) collective-permute-start(bf16[1,320,128]{2,1,0:T(8,128)(2,1)S(1)} %fusion.17), channel_id=1, source_target_pairs={{1,0},{2,1},{3,2},{5,4},{6,5},{7,6},{9,8},{10,9},{11,10},{13,12},{... | collective-permute-start | bytes 245768 | tf_op jit(solution)/shard_map/ppermute | solution.py:24
  9.4 8.9 %collective-permute-start = (bf16[1,320,128]{2,1,0:T(8,128)(2,1)S(1)}, bf16[1,320,128]{2,1,0:T(8,128)(2,1)S(1)}, u32[]{:S(2)}, u32[]{:S(2)}) collective-permute-start(bf16[1,320,128]{2,1,0:T(8,128)(2,1)S(1)} %fusion.17), channel_id=1, source_target_pairs={{0,1},{1,2},{2,3},{4,5},{5,6},{6,7},{8,9},{9,10},{10,11},{12,13},{... | collective-permute-start | bytes 245768 | tf_op jit(solution)/shard_map/ppermute | solution.py:22
  20.0 0.9 copy-start.1
  34.4 83.7 %all-to-all-start = ((bf16[128,4,2880]{2,1,0:T(4,128)(2,1)}), bf16[128,4,2880]{2,1,0:T(4,128)(2,1)S(1)}, u32[]{:S(2)}, u32[]{:S(2)}) async-start(bf16[128,4,2880]{2,1,0:T(4,128)(2,1)} %select_convert_fusion), calls=%async_computation | async-start | bytes 6029312 | tf_op jit(solution)/shard_map/all_to_all | solution.py:109
  47.9 96.6 %copy-start.5 = (f32[4,2880]{1,0:T(4,128)S(1)}, f32[4,2880]{1,0:T(4,128)}, u32[]{:S(2)}) copy-start(f32[4,2880]{1,0:T(4,128)} %param.10) | copy-start | bytes 138244
  48.0 96.6 %copy-start.6 = (f32[4,2880]{1,0:T(4,128)S(1)}, f32[4,2880]{1,0:T(4,128)}, u32[]{:S(2)}) copy-start(f32[4,2880]{1,0:T(4,128)} %param.12) | copy-start | bytes 138244
  48.0 96.6 %copy-start.7 = (f32[4,2880]{1,0:T(4,128)S(1)}, f32[4,2880]{1,0:T(4,128)}, u32[]{:S(2)}) copy-start(f32[4,2880]{1,0:T(4,128)} %param.11) | copy-start | bytes 138244
  48.0 97.3 %copy-start.3 = (bf16[1,1,320,128]{3,2,1,0:T(8,128)(2,1)S(1)}, bf16[1,1,320,128]{3,2,1,0:T(8,128)(2,1)}, u32[]{:S(2)}) copy-start(bf16[1,1,320,128]{3,2,1,0:T(8,128)(2,1)} %param.8) | copy-start | bytes 245764
  48.0 112.4 %all-gather.4.cloned.1.call-start = ((), (), s32[]{:S(2)}) async-start(), calls=%async_computation.1 | async-start | bytes 2355200 | tf_op jit(solution)/shard_map/all_gather | solution.py:74
  48.7 309.9 %all-gather.6.cloned.1.call-start = ((), (), s32[]{:S(2)}) async-start(), calls=%async_computation.2 | async-start | bytes 3038208 | tf_op jit(solution)/shard_map/all_gather | solution.py:122
  145.3 7.2 %collective-permute-start.3 = (bf16[1,320,128]{2,1,0:T(8,128)(2,1)S(1)}, bf16[1,320,128]{2,1,0:T(8,128)(2,1)S(1)}, u32[]{:S(2)}, u32[]{:S(2)}) collective-permute-start(bf16[1,320,128]{2,1,0:T(8,128)(2,1)S(1)} %bitcast.61), channel_id=1, source_target_pairs={{1,0},{2,1},{3,2},{5,4},{6,5},{7,6},{9,8},{10,9},{11,10},{13,12},{... | collective-permute-start | bytes 245768 | tf_op jit(solution)/shard_map/ppermute | solution.py:24
  146.6 7.5 %collective-permute-start.2 = (bf16[1,320,128]{2,1,0:T(8,128)(2,1)S(1)}, bf16[1,320,128]{2,1,0:T(8,128)(2,1)S(1)}, u32[]{:S(2)}, u32[]{:S(2)}) collective-permute-start(bf16[1,320,128]{2,1,0:T(8,128)(2,1)S(1)} %bitcast.62), channel_id=1, source_target_pairs={{0,1},{1,2},{2,3},{4,5},{5,6},{6,7},{8,9},{9,10},{10,11},{12,13},{... | collective-permute-start | bytes 245768 | tf_op jit(solution)/shard_map/ppermute | solution.py:22
  163.7 2.5 copy-start.2
  163.7 2.5 copy-start.4
  166.2 3.0 copy-start
Sparse Core Ops, SparseCore 0:
  50.9 76.2 all-gather.3
  145.4 213.1 all-gather.5
where the time goes:
time: 372 us; the launch traced here: 371 us
  waiting for transfers between devices  258 us (69%)
  starting transfers between devices  28.5 us (8%)
  local copies, waits for them, and re-layouts  27.6 us (7%)
  blocking collectives  25.1 us (7%)
  between operations  14.3 us (4%)
  other arithmetic  10.2 us (3%)
  matrix products  7.22 us (2%)
    all_gather x1, waiting for transfers between devices, local(): lax.all_gather(new_master.astype(jnp.bfloat16), 'dp', axis=0, tiled=True)  187 us
    all_to_all x1, waiting for transfers between devices, local(): lax.all_to_all(outgoing.astype(jnp.bfloat16), 'dp', split_axis=0, concat_...  69.2 us
    psum x1, blocking collectives, local(): lax.psum(jnp.sum(incoming, axis=0).astype(jnp.bfloat16), 'strip')  25.1 us
    all_to_all x1, starting transfers between devices, local(): lax.all_to_all(outgoing.astype(jnp.bfloat16), 'dp', split_axis=0, concat_...  13.5 us
    ppermute x2, starting transfers between devices, extended(): lax.ppermute(tail, axis, [(i, (i + 1) % count) for i in range(ends)])  12.3 us
    unnamed x32, local copies, waits for them, and re-layouts  10.9 us
    gather x2, local copies, waits for them, and re-layouts, local(): jnp.take(partial_grad, source_row, axis=0, mode='fill', fill_value=0.0)  8.37 us
  transfers between devices with their start and end apart: 7, of which 4 were waited for; matrix products, arithmetic and copies ran while one was open for 6% of the time, Pallas kernels for 0%

commit v1 on v0

--- a/solution.py
+++ b/solution.py
@@ -119,7 +119,12 @@
     new_master, new_first, new_second = adam_update(
         gradient, master, first_moment, second_moment, my_filled
     )
-    published = lax.all_gather(new_master.astype(jnp.bfloat16), "dp", axis=0, tiled=True)
+    published = jnp.concatenate(
+        lax.all_to_all(
+            jnp.stack([new_master.astype(jnp.bfloat16)] * lax.axis_size("dp")), "dp", 0, 0
+        ),
+        axis=0,
+    )
     quarter = weight.shape[0]
     wanted = lax.dynamic_slice_in_dim(slot_ids, lax.axis_index("strip") * quarter, quarter)
     new_weight = published[wanted]

time: 372 us -> 255 us (0.69)
  the two profiles are of different devices: /device:TPU:8 before, /device:TPU:1 now
where the time goes in v1:
time: 255 us; the launch traced here: 254 us
  waiting for transfers between devices  129 us (51%)
  starting transfers between devices  42.1 us (17%)
  local copies, waits for them, and re-layouts  30.1 us (12%)
  blocking collectives  20.8 us (8%)
  between operations  14.3 us (6%)
  other arithmetic  10.2 us (4%)
  matrix products  7.21 us (3%)
    all_to_all x1, waiting for transfers between devices, local(): lax.all_to_all(outgoing.astype(jnp.bfloat16), 'dp', split_axis=0, concat_...  69.1 us
    all_gather x1, waiting for transfers between devices, local(): full_weight = lax.all_gather(weight, 'strip', axis=0, tiled=True)  57.6 us
    psum x1, blocking collectives, local(): lax.psum(jnp.sum(incoming, axis=0).astype(jnp.bfloat16), 'strip')  20.8 us
    all_to_all x1, starting transfers between devices, local(): lax.all_to_all(outgoing.astype(jnp.bfloat16), 'dp', split_axis=0, concat_...  14 us
    all_to_all x1, starting transfers between devices, local(): lax.all_to_all(jnp.stack([new_master.astype(jnp.bfloat16)] * lax.axis_siz...  13.3 us
    ppermute x2, starting transfers between devices, extended(): lax.ppermute(tail, axis, [(i, (i + 1) % count) for i in range(ends)])  12.1 us
    gather x2, local copies, waits for them, and re-layouts, local(): jnp.take(partial_grad, source_row, axis=0, mode='fill', fill_value=0.0)  8.37 us
    unnamed x31, local copies, waits for them, and re-layouts  6.55 us
  transfers between devices with their start and end apart: 7, of which 4 were waited for; matrix products, arithmetic and copies ran while one was open for 8% of the time, Pallas kernels for 0%

profile of v1, /device:TPU:1, one launch (start us, length us, event | category | flops | bytes accessed | tf_op | source)
XLA Modules:
  0.0 253.7 jit_solution(17353990538246742195)
XLA Ops:
  7.2 0.9 fusion.17
  8.1 1.3 collective-permute-start.1
  9.4 7.3 %collective-permute-start = (bf16[1,320,128]{2,1,0:T(8,128)(2,1)S(1)}, bf16[1,320,128]{2,1,0:T(8,128)(2,1)S(1)}, u32[]{:S(2)}, u32[]{:S(2)}) collective-permute-start(bf16[1,320,128]{2,1,0:T(8,128)(2,1)S(1)} %fusion.17), channel_id=1, source_target_pairs={{0,1},{1,2},{2,3},{4,5},{5,6},{6,7},{8,9},{9,10},{10,11},{12,13},{... | collective-permute-start | bytes 245768 | tf_op jit(solution)/shard_map/ppermute | solution.py:22
  16.7 1.0 convert_reduce_fusion
  17.7 0.7 multiply_add_fusion
  18.3 0.2 fusion.11
  18.5 0.1 select_reduce_fusion
  18.7 0.1 select_n.68
  18.9 0.2 select_maximum_fusion.2
  19.1 0.1 slice_dynamic-update-slice_fusion.10
  19.3 1.0 constant_dynamic-update-slice_fusion.1
  20.2 0.1 slice_dynamic-update-slice_fusion.8
  20.4 0.1 slice_dynamic-update-slice_fusion.6
  20.5 0.9 copy-done.1
  21.4 1.5 convolution_bitcast_fusion
  22.9 3.7 %gather_fusion = bf16[512,2880]{1,0:T(8,128)(2,1)} fusion(bf16[320,2880]{1,0:T(8,128)(2,1)S(1)} %convolution_bitcast_fusion, s32[1024]{0:T(1024)S(1)} %pad_clamp_fusion.1), kind=kCustom, calls=%fused_computation | custom fusion | bytes 5900288 | tf_op jit(solution)/shard_map/jit(_take)/gather | solution.py:106
  26.6 4.7 %gather.10 = bf16[128,4,2880]{2,1,0:T(4,128)(2,1)S(1)} reshape(bf16[512,2880]{1,0:T(8,128)(2,1)} %gather_fusion) | data formatting | bytes 5898240 | tf_op jit(solution)/shard_map/jit(_take)/gather | solution.py:106
  31.3 3.7 %select_convert_fusion = bf16[128,4,2880]{2,1,0:T(4,128)(2,1)} fusion(bf16[128,4,2880]{2,1,0:T(4,128)(2,1)S(1)} %gather.10, pred[128,4]{1,0:T(8,128)(4,1)S(1)} %compare_and_fusion), kind=kLoop, calls=%fused_computation.2 | loop fusion | flops 1474560 | bytes 5898752 | tf_op jit(solution)/shard_map/convert_element_type | solution.py:110
  35.0 14.0 %all-to-all-start = ((bf16[128,4,2880]{2,1,0:T(4,128)(2,1)}), bf16[128,4,2880]{2,1,0:T(4,128)(2,1)S(1)}, u32[]{:S(2)}, u32[]{:S(2)}) async-start(bf16[128,4,2880]{2,1,0:T(4,128)(2,1)} %select_convert_fusion), calls=%async_computation | async-start | bytes 6029312 | tf_op jit(solution)/shard_map/all_to_all | solution.py:109
  49.1 0.1 dynamic_slice.6
  49.1 69.1 %all-to-all-done = bf16[128,4,2880]{2,1,0:T(4,128)(2,1)S(1)} async-done(((bf16[128,4,2880]{2,1,0:T(4,128)(2,1)}), bf16[128,4,2880]{2,1,0:T(4,128)(2,1)S(1)}, u32[]{:S(2)}, u32[]{:S(2)}) %all-to-all-start) | async-done | bytes 2949152 | tf_op jit(solution)/shard_map/all_to_all | solution.py:109
  118.2 1.3 reduce_sum.32
  119.5 20.8 %psum.7 = bf16[4,2880]{1,0:T(4,128)(2,1)S(1)} all-reduce(bf16[4,2880]{1,0:T(4,128)(2,1)S(1)} %reduce_sum.32), channel_id=1, replica_groups=mesh['dp'=128,'strip'=4] {'strip'}, use_global_device_ids=true, to_apply=%region_4.5 | all-reduce | flops 11520 | bytes 46080 | tf_op jit(solution)/shard_map/psum | solution.py:112
  140.3 0.8 fusion.26
  141.0 2.4 stack.2
  143.5 13.3 %all-to-all-start.1 = ((bf16[128,4,2880]{2,1,0:T(4,128)(2,1)}), bf16[128,4,2880]{2,1,0:T(4,128)(2,1)}, u32[]{:S(2)}, u32[]{:S(2)}) async-start(bf16[128,4,2880]{2,1,0:T(4,128)(2,1)} %stack.2), calls=%async_computation.1 | async-start | bytes 6029312 | tf_op jit(solution)/shard_map/all_to_all | solution.py:123
  156.8 0.7 all-gather.2.cloned.1.call-update
  157.5 1.3 collective-permute-start.3
  158.8 4.9 %collective-permute-start.2 = (bf16[1,320,128]{2,1,0:T(8,128)(2,1)S(1)}, bf16[1,320,128]{2,1,0:T(8,128)(2,1)S(1)}, u32[]{:S(2)}, u32[]{:S(2)}) collective-permute-start(bf16[1,320,128]{2,1,0:T(8,128)(2,1)S(1)} %bitcast.60), channel_id=1, source_target_pairs={{0,1},{1,2},{2,3},{4,5},{5,6},{6,7},{8,9},{9,10},{10,11},{12,13},{... | collective-permute-start | bytes 245768 | tf_op jit(solution)/shard_map/ppermute | solution.py:22
  163.8 0.6 collective-permute-done.3
  164.4 1.1 collective-permute-done.2
  165.5 0.2 select_maximum_fusion
  165.8 0.7 slice_dynamic-update-slice_fusion.5
  166.5 0.6 constant_dynamic-update-slice_fusion.5
  167.1 0.7 slice_dynamic-update-slice_fusion.4
  167.8 0.7 slice_dynamic-update-slice_fusion.3
  168.5 0.6 constant_dynamic-update-slice_fusion.4
  169.1 0.6 slice_dynamic-update-slice_fusion.2
  169.8 0.7 slice_dynamic-update-slice_fusion.1
  170.5 0.6 constant_dynamic-update-slice_fusion.3
  171.1 0.6 slice_dynamic-update-slice_fusion
  171.7 57.6 %all-gather.2.cloned.1.call-done = bf16[320,2880]{1,0:T(8,128)(2,1)} async-done(((bf16[80,2880]{1,0:T(8,128)(2,1)}), bf16[320,2880]{1,0:T(8,128)(2,1)}) %all-gather.2.cloned.1.call-update) | async-done | bytes 1843216 | tf_op jit(solution)/shard_map/all_gather | solution.py:74
  229.3 3.3 %copy.17 = bf16[320,2880]{0,1:T(8,128)(2,1)S(1)} copy(bf16[320,2880]{1,0:T(8,128)(2,1)} %all-gather.2.cloned.1.call-done) | data formatting | bytes 3686400 | tf_op jit(solution)/shard_map/all_gather | solution.py:74
  232.6 2.5 copy.18
  235.2 3.0 %fusion.6 = bf16[1,1,320,128]{3,2,1,0:T(8,128)(2,1)} fusion(bf16[320,2880]{1,0:T(8,128)(2,1)} %all-gather.2.cloned.1.call-done, bf16[1,2880,128]{2,1,0:T(8,128)(2,1)S(1)} %copy-done.2, bf16[1,1,320,128]{3,2,1,0:T(8,128)(2,1)S(1)} %copy-done.4), kind=kOutput, calls=%fused_computation.14 | convolution fusion | flops 236052480 | bytes 2744320 | tf_op jit(solution)/shard_map/ok,hkw->how/dot_general | solution.py:82
  238.1 2.7 %fusion.5 = bf16[1,1,320,128]{3,2,1,0:T(8,128)(2,1)} fusion(bf16[320,2880]{0,1:T(8,128)(2,1)S(1)} %bitcast.58, bf16[1,2880,128]{2,1,0:T(8,128)(2,1)} %slice_dynamic-update-slice_fusion, bf16[1,1,320,128]{3,2,1,0:T(8,128)(2,1)S(1)} %copy-done.4, bf16[1,1,320,128]{3,2,1,0:T(8,128)(2,1)S(1)} %copy-done.3), kind=kOutput, calls=%fused_computation.13 | convolution fusion | flops 236421120 | bytes 2826240 | tf_op jit(solution)/shard_map/ck,hkw->hcw/dot_general | solution.py:88
  240.8 4.4 %reshape.157 = bf16[512,2880]{1,0:T(8,128)(2,1)S(1)} reshape(bf16[128,4,2880]{2,1,0:T(4,128)(2,1)} %all-to-all-done.1) | data formatting | bytes 5898240 | tf_op jit(solution)/shard_map/reshape | solution.py:122
  245.2 1.6 gather_fusion.1
  (30 shorter events, 0.3 us)
Async XLA Ops:
  8.1 10.7 %collective-permute-start.1 = (bf16[1,320,128]{2,1,0:T(8,128)(2,1)S(1)}, bf16[1,320,128]{2,1,0:T(8,128)(2,1)S(1)}, u32[]{:S(2)}, u32[]{:S(2)}) collective-permute-start(bf16[1,320,128]{2,1,0:T(8,128)(2,1)S(1)} %fusion.17), channel_id=1, source_target_pairs={{1,0},{2,1},{3,2},{5,4},{6,5},{7,6},{9,8},{10,9},{11,10},{13,12},{... | collective-permute-start | bytes 245768 | tf_op jit(solution)/shard_map/ppermute | solution.py:24
  9.4 9.4 %collective-permute-start = (bf16[1,320,128]{2,1,0:T(8,128)(2,1)S(1)}, bf16[1,320,128]{2,1,0:T(8,128)(2,1)S(1)}, u32[]{:S(2)}, u32[]{:S(2)}) collective-permute-start(bf16[1,320,128]{2,1,0:T(8,128)(2,1)S(1)} %fusion.17), channel_id=1, source_target_pairs={{0,1},{1,2},{2,3},{4,5},{5,6},{6,7},{8,9},{9,10},{10,11},{12,13},{... | collective-permute-start | bytes 245768 | tf_op jit(solution)/shard_map/ppermute | solution.py:22
  20.5 0.9 copy-start.1
  35.0 83.2 %all-to-all-start = ((bf16[128,4,2880]{2,1,0:T(4,128)(2,1)}), bf16[128,4,2880]{2,1,0:T(4,128)(2,1)S(1)}, u32[]{:S(2)}, u32[]{:S(2)}) async-start(bf16[128,4,2880]{2,1,0:T(4,128)(2,1)} %select_convert_fusion), calls=%async_computation | async-start | bytes 6029312 | tf_op jit(solution)/shard_map/all_to_all | solution.py:109
  49.0 91.2 %copy-start.5 = (f32[4,2880]{1,0:T(4,128)S(1)}, f32[4,2880]{1,0:T(4,128)}, u32[]{:S(2)}) copy-start(f32[4,2880]{1,0:T(4,128)} %param.10) | copy-start | bytes 138244
  49.0 91.2 %copy-start.6 = (f32[4,2880]{1,0:T(4,128)S(1)}, f32[4,2880]{1,0:T(4,128)}, u32[]{:S(2)}) copy-start(f32[4,2880]{1,0:T(4,128)} %param.12) | copy-start | bytes 138244
  49.0 91.2 %copy-start.7 = (f32[4,2880]{1,0:T(4,128)S(1)}, f32[4,2880]{1,0:T(4,128)}, u32[]{:S(2)}) copy-start(f32[4,2880]{1,0:T(4,128)} %param.11) | copy-start | bytes 138244
  143.5 14.0 %copy-start.3 = (bf16[1,1,320,128]{3,2,1,0:T(8,128)(2,1)S(1)}, bf16[1,1,320,128]{3,2,1,0:T(8,128)(2,1)}, u32[]{:S(2)}) copy-start(bf16[1,1,320,128]{3,2,1,0:T(8,128)(2,1)} %param.8) | copy-start | bytes 245764
  143.5 97.4 %all-to-all-start.1 = ((bf16[128,4,2880]{2,1,0:T(4,128)(2,1)}), bf16[128,4,2880]{2,1,0:T(4,128)(2,1)}, u32[]{:S(2)}, u32[]{:S(2)}) async-start(bf16[128,4,2880]{2,1,0:T(4,128)(2,1)} %stack.2), calls=%async_computation.1 | async-start | bytes 6029312 | tf_op jit(solution)/shard_map/all_to_all | solution.py:123
  156.8 72.5 %all-gather.2.cloned.1.call-start = ((), (), s32[]{:S(2)}) async-start(), calls=%async_computation.2 | async-start | bytes 2355200 | tf_op jit(solution)/shard_map/all_gather | solution.py:74
  157.5 6.9 %collective-permute-start.3 = (bf16[1,320,128]{2,1,0:T(8,128)(2,1)S(1)}, bf16[1,320,128]{2,1,0:T(8,128)(2,1)S(1)}, u32[]{:S(2)}, u32[]{:S(2)}) collective-permute-start(bf16[1,320,128]{2,1,0:T(8,128)(2,1)S(1)} %bitcast.59), channel_id=1, source_target_pairs={{1,0},{2,1},{3,2},{5,4},{6,5},{7,6},{9,8},{10,9},{11,10},{13,12},{... | collective-permute-start | bytes 245768 | tf_op jit(solution)/shard_map/ppermute | solution.py:24
  158.8 6.7 %collective-permute-start.2 = (bf16[1,320,128]{2,1,0:T(8,128)(2,1)S(1)}, bf16[1,320,128]{2,1,0:T(8,128)(2,1)S(1)}, u32[]{:S(2)}, u32[]{:S(2)}) collective-permute-start(bf16[1,320,128]{2,1,0:T(8,128)(2,1)S(1)} %bitcast.60), channel_id=1, source_target_pairs={{0,1},{1,2},{2,3},{4,5},{5,6},{6,7},{8,9},{9,10},{10,11},{12,13},{... | collective-permute-start | bytes 245768 | tf_op jit(solution)/shard_map/ppermute | solution.py:22
  232.6 2.5 %copy-start.2 = (bf16[1,2880,128]{2,1,0:T(8,128)(2,1)S(1)}, bf16[1,2880,128]{2,1,0:T(8,128)(2,1)}, u32[]{:S(2)}) copy-start(bf16[1,2880,128]{2,1,0:T(8,128)(2,1)} %copy-done.1) | copy-start | bytes 2211844
  232.6 2.5 copy-start.4
  235.2 3.0 %copy-start = (bf16[320,9,320]{0,2,1:T(8,128)(2,1)S(1)}, bf16[320,9,320]{0,2,1:T(8,128)(2,1)}, u32[]{:S(2)}) copy-start(bf16[320,9,320]{0,2,1:T(8,128)(2,1)} %copy.18) | copy-start | bytes 5529604
Sparse Core Ops, SparseCore 0:
  159.7 69.5 all-gather.1
